TPU v7x, 32 devices: a whole 2x2x4 slice. The times are simulated.
32 devices in a mesh: seq: 4 (over z), chan: 4 (over y, core), rep: 2 (over x).
Axes of the slice: x: 2, y: 2, z: 4, core: 2. Of those that a mesh axis runs over, the one named last changes fastest.
Arguments:
- inputs: float32 [2, 4096, 512], P('rep', 'chan', 'seq'), may hold values from -0.25 to 0.25
- out_grad: float32 [2, 4096, 512], P('rep', 'chan', 'seq'), may hold values from -6 to 6
- filters: float32 [4, 1024, 512], P('chan', 'seq'), may hold values from -0.25 to 0.25
- segment_ids: int32 [2, 512], P('rep'), may hold values from 0 to 1, as said below
Outputs:
- input_grad: float32 [2, 4096, 512], P('rep', 'chan', 'seq')
- filter_grad: float32 [4, 1024, 512], P('chan', 'seq')
Inputs may be any that keep to these rules, and one draw needn't show every extreme that they name: `segment_ids`: in each replica's row the ids are 0 up to some position and 1 from it on; that position lies between 64 and 448.
All inputs are finite; a program needn't handle non-finite values.
Results may differ from a plain program's by a relative error of at most 0.000098.
Values sent between devices are 32-bit elements; how exact they have to be, the bound alone decides.
A program may use at most 64 MiB of HBM per device.

v0:
```python
import math
import jax
import jax.numpy as jnp
from jax import lax
from jax.sharding import PartitionSpec as P


def table_pair(row_count, col_count, period):
    row_index = jnp.arange(row_count, dtype=jnp.int32)[:, None]
    col_index = jnp.arange(col_count, dtype=jnp.int32)[None, :]
    phases = row_index * col_index % period
    angles = phases.astype(jnp.float32) * (2.0 * math.pi / period)
    return (jnp.cos(angles), -jnp.sin(angles))


def contract(formula, left_part, right_part):
    return jnp.einsum(
        formula,
        left_part,
        right_part,
        precision=lax.Precision.HIGHEST,
        preferred_element_type=jnp.float32,
    )


def make_tables(length):
    full_len = 2 * length
    col_size = 128
    row_size = full_len // col_size
    half_rows = row_size // 2
    outer_cos, outer_sin = table_pair(row_size, row_size, row_size)
    fwd_cos = outer_cos[:, :half_rows]
    fwd_sin = outer_sin[:, :half_rows]
    outer_fwd = jnp.concatenate(
        [jnp.concatenate([fwd_cos, -fwd_sin], axis=1), jnp.concatenate([fwd_sin, fwd_cos], axis=1)],
        axis=0,
    )
    inv_cos = outer_cos[:half_rows]
    inv_sin = outer_sin[:half_rows]
    outer_inv = jnp.concatenate(
        [jnp.concatenate([inv_cos, inv_sin], axis=1), jnp.concatenate([-inv_sin, inv_cos], axis=1)],
        axis=0,
    )
    twiddle = table_pair(row_size, col_size, full_len)
    inner_cos, inner_sin = table_pair(col_size, col_size, col_size)
    inner_fwd = jnp.stack(
        [jnp.stack([inner_cos, inner_sin], axis=1), jnp.stack([-inner_sin, inner_cos], axis=1)],
        axis=0,
    )
    inner_inv = jnp.stack(
        [jnp.stack([inner_cos, -inner_sin], axis=1), jnp.stack([inner_sin, inner_cos], axis=1)],
        axis=0,
    )
    return (outer_fwd, outer_inv, twiddle, inner_fwd, inner_inv, half_rows, col_size)


def forward_spectrum(signal, real_only, tables):
    outer_fwd, outer_inv, twiddle, inner_fwd, inner_inv, half_rows, col_size = tables
    chan_count = signal.shape[0]
    if real_only:
        section = contract("ja,cab->cjb", outer_fwd[:, :half_rows], signal)
    else:
        section = contract(
            "ja,cab->cjb", outer_fwd, signal.reshape(chan_count, 2 * half_rows, col_size)
        )
    section = section.reshape(chan_count, 2, 2 * half_rows, col_size)
    section_re = section[:, 0]
    section_im = section[:, 1]
    turned = jnp.stack(
        [
            section_re * twiddle[0] - section_im * twiddle[1],
            section_re * twiddle[1] + section_im * twiddle[0],
        ],
        axis=1,
    )
    return contract("cpjb,pbqm->cqjm", turned, inner_fwd)


def inverse_signal(spectrum, tables, want_imag):
    outer_fwd, outer_inv, twiddle, inner_fwd, inner_inv, half_rows, col_size = tables
    chan_count = spectrum.shape[0]
    factor = 1.0 / (2 * half_rows * col_size)
    mixed = contract("cqjm,qmpb->cpjb", spectrum, inner_inv)
    mixed_re = mixed[:, 0]
    mixed_im = mixed[:, 1]
    turned = jnp.stack(
        [
            mixed_re * twiddle[0] + mixed_im * twiddle[1],
            mixed_im * twiddle[0] - mixed_re * twiddle[1],
        ],
        axis=1,
    )
    turned = turned.reshape(chan_count, 4 * half_rows, col_size)
    table = outer_inv if want_imag else outer_inv[:half_rows]
    signal = contract("aj,cjb->cab", table, turned) * factor
    return signal.reshape(chan_count, -1, half_rows, col_size)


def conj_product(left_spec, right_spec):
    left_re = left_spec[:, 0]
    left_im = left_spec[:, 1]
    right_re = right_spec[:, 0]
    right_im = right_spec[:, 1]
    return jnp.stack(
        [left_re * right_re + left_im * right_im, left_re * right_im - left_im * right_re], axis=1
    )


def pair_spectrum(whole, first_mask, second_mask, tables):
    signal = whole.reshape(-1, tables[5], tables[6])
    packed = jnp.stack([signal * first_mask, signal * second_mask], axis=1)
    return forward_spectrum(packed, False, tables)


def return_grad(filter_spec, grad_spec, first_mask, second_mask, tables, slab_width, tok_count):
    product = conj_product(filter_spec, grad_spec)
    back = inverse_signal(product, tables, True)
    grad_full = first_mask * back[:, 0] + second_mask * back[:, 1]
    chan_count = grad_full.shape[0]
    pieces = grad_full.reshape(1, chan_count, -1)
    returned = lax.all_to_all(pieces, "seq", split_axis=2, concat_axis=0, tiled=True)
    return returned.reshape(1, slab_width, tok_count)


def sum_filter_grad(act_spec, grad_spec, tables):
    product = conj_product(act_spec, grad_spec)
    signal_re = inverse_signal(product, tables, False)
    chan_count = signal_re.shape[0]
    return lax.psum(signal_re.reshape(1, chan_count, -1), "rep")


def body(inputs, out_grad, filters, segment_ids):
    seq_count = lax.axis_size("seq")
    slab_width = inputs.shape[1]
    tok_count = inputs.shape[2]
    chan_count = slab_width // seq_count
    length = tok_count * seq_count
    tables = make_tables(length)
    half_rows = tables[5]
    col_size = tables[6]
    second_mask = segment_ids[0].astype(jnp.float32).reshape(half_rows, col_size)
    first_mask = 1.0 - second_mask
    filter_spec = forward_spectrum(
        filters[0].reshape(chan_count, half_rows, col_size), True, tables
    )
    act_pieces = inputs.reshape(seq_count, chan_count, tok_count)
    grad_pieces = out_grad.reshape(seq_count, chan_count, tok_count)
    act_whole, grad_whole = (
        lax.all_to_all(act_pieces, "seq", split_axis=0, concat_axis=2, tiled=True),
        lax.all_to_all(grad_pieces, "seq", split_axis=0, concat_axis=2, tiled=True),
    )
    grad_spec = pair_spectrum(grad_whole, first_mask, second_mask, tables)
    input_grad = return_grad(
        filter_spec, grad_spec, first_mask, second_mask, tables, slab_width, tok_count
    )
    act_spec = pair_spectrum(act_whole, first_mask, second_mask, tables)
    filter_grad = sum_filter_grad(act_spec, grad_spec, tables)
    return (input_grad, filter_grad)


def solution(mesh):
    return jax.shard_map(
        body,
        mesh=mesh,
        in_specs=(
            P("rep", "chan", "seq"),
            P("rep", "chan", "seq"),
            P("chan", "seq", None),
            P("rep", None),
        ),
        out_specs=(P("rep", "chan", "seq"), P("chan", "seq", None)),
        check_vma=False,
    )
```

profile of v0, /device:TPU:0, one launch (start us, length us, event | category | flops | bytes accessed | tf_op | source)
XLA Modules:
  0.0 125.6 jit_solution(4370979219491827914)
XLA Ops:
  7.2 6.4 %all-to-all-start = ((f32[4,256,128]{2,1,0:T(8,128)}), f32[4,256,128]{2,1,0:T(8,128)S(1)}, u32[]{:S(2)}, u32[]{:S(2)}) async-start(f32[4,256,128]{2,1,0:T(8,128)} %bitcast.152), calls=%async_computation | async-start | bytes 1048576 | tf_op jit(solution)/shard_map/all_to_all | solution.py:150
  14.2 1.2 reshape_squeeze.3
  16.8 1.9 %convolution_bitcast_fusion = f32[256,2,8,128]{3,2,1,0:T(8,128)S(1)} fusion(f32[256,4,128]{2,1,0:T(4,128)S(1)} %reshape_squeeze.3, f32[16,8]{0,1:T(8,128)S(1)} %maximum_maximum_fusion), kind=kOutput, calls=%fused_computation.26 | convolution fusion | flops 25165824 | bytes 2623488 | tf_op jit(solution)/shard_map/ja,cab->cjb/dot_general | solution.py:17
  18.6 9.4 %all-to-all-done = f32[4,256,128]{2,1,0:T(8,128)S(1)} async-done(((f32[4,256,128]{2,1,0:T(8,128)}), f32[4,256,128]{2,1,0:T(8,128)S(1)}, u32[]{:S(2)}, u32[]{:S(2)}) %all-to-all-start) | async-done | bytes 524320 | tf_op jit(solution)/shard_map/all_to_all | solution.py:150
  28.0 4.3 %all-to-all-start.2 = ((f32[4,256,128]{2,1,0:T(8,128)}), f32[4,256,128]{2,1,0:T(8,128)}, u32[]{:S(2)}, u32[]{:S(2)}) async-start(f32[4,256,128]{2,1,0:T(8,128)} %bitcast.153), calls=%async_computation.2 | async-start | bytes 1048576 | tf_op jit(solution)/shard_map/all_to_all | solution.py:149
  33.7 1.3 %copy.72 = f32[4,8]{1,0:T(4,128)} copy(f32[4,8]{0,1:T(8,128)} %bitcast.159) | data formatting | bytes 256 | tf_op jit(solution)/shard_map/slice | solution.py:38
  38.1 8.2 %all-to-all-done.2 = f32[4,256,128]{2,1,0:T(8,128)} async-done(((f32[4,256,128]{2,1,0:T(8,128)}), f32[4,256,128]{2,1,0:T(8,128)}, u32[]{:S(2)}, u32[]{:S(2)}) %all-to-all-start.2) | async-done | bytes 524320 | tf_op jit(solution)/shard_map/all_to_all | solution.py:149
  46.3 1.5 %bitcast_multiply_fusion.5 = (f32[256,1,4,128]{3,0,2,1:T(8,128)S(1)}, f32[256,1,4,128]{3,0,2,1:T(8,128)S(1)}, f32[256,1,4,128]{3,0,2,1:T(8,128)S(1)}, f32[256,1,4,128]{3,0,2,1:T(8,128)S(1)}) fusion(f32[4,256,128]{2,1,0:T(8,128)} %copy-done.1, f32[4,128]{1,0:T(4,128)} %broadcast_subtract_fusion, f32[4,128]{1,0:T(4,128)S(1)} %bitcast.157, ...), kind=kLoop, calls=%fused_computation.59 | loop fusion | flops 524288 | bytes 3149824 | tf_op jit(solution)/shard_map/mul | solution.py:111
  48.6 1.9 %convolution_bitcast_fusion.2 = f32[256,2,8,128]{3,2,1,0:T(8,128)S(1)} fusion(f32[256,8,128]{2,1,0:T(8,128)S(1)} %bitcast.150, f32[16,8]{0,1:T(8,128)S(1)} %maximum_maximum_fusion), kind=kOutput, calls=%fused_computation.31 | convolution fusion | flops 50331648 | bytes 3146240 | tf_op jit(solution)/shard_map/ja,cab->cjb/dot_general | solution.py:17
  51.3 1.9 %convolution_bitcast_fusion.1 = f32[256,2,8,128]{3,2,1,0:T(8,128)S(1)} fusion(f32[256,8,128]{2,1,0:T(8,128)S(1)} %bitcast.149, f32[16,8]{0,1:T(8,128)S(1)} %maximum_maximum_fusion), kind=kOutput, calls=%fused_computation.30 | convolution fusion | flops 50331648 | bytes 3146240 | tf_op jit(solution)/shard_map/ja,cab->cjb/dot_general | solution.py:17
  54.4 1.2 multiply_subtract_fusion.2
  55.6 2.0 %fusion.21 = f32[256,2,8,128]{0,3,2,1:T(8,128)S(1)} fusion(f32[256,1,8,128]{3,0,1,2:T(8,128)S(1)} %get-tuple-element.40, f32[256,1,8,128]{3,0,1,2:T(8,128)S(1)} %get-tuple-element.41, f32[1,128,2,128]{1,3,0,2:T(8,128)S(1)} %get-tuple-element.31, f32[1,128,2,128]{1,3,0,2:T(8,128)S(1)} %get-tuple-element.34), kind=kOutput, calls=%fused_computation.29 | convolution fusion | flops 1611202560 | bytes 4456448 | tf_op jit(solution)/shard_map/cpjb,pbqm->cqjm/dot_general | solution.py:17
  57.6 2.0 %fusion.20 = f32[256,2,8,128]{0,3,2,1:T(8,128)S(1)} fusion(f32[256,1,8,128]{3,0,1,2:T(8,128)S(1)} %get-tuple-element.38, f32[256,1,8,128]{3,0,1,2:T(8,128)S(1)} %get-tuple-element.39, f32[1,128,2,128]{1,3,0,2:T(8,128)S(1)} %get-tuple-element.31, f32[1,128,2,128]{1,3,0,2:T(8,128)S(1)} %get-tuple-element.34), kind=kOutput, calls=%fused_computation.28 | convolution fusion | flops 1611202560 | bytes 4456448 | tf_op jit(solution)/shard_map/cpjb,pbqm->cqjm/dot_general | solution.py:17
  59.5 2.2 %fusion.19 = f32[256,2,8,128]{0,3,2,1:T(8,128)S(1)} fusion(f32[256,1,8,128]{3,0,1,2:T(8,128)S(1)} %get-tuple-element.9, f32[256,1,8,128]{3,0,1,2:T(8,128)S(1)} %get-tuple-element.8, f32[1,128,2,128]{1,3,0,2:T(8,128)S(1)} %get-tuple-element.31, f32[1,128,2,128]{1,3,0,2:T(8,128)S(1)} %get-tuple-element.34), kind=kOutput, calls=%fused_computation.27 | convolution fusion | flops 1611202560 | bytes 4456448 | tf_op jit(solution)/shard_map/cpjb,pbqm->cqjm/dot_general | solution.py:17
  62.6 3.6 %fusion.22 = f32[256,2,8,128]{3,0,1,2:T(8,128)S(1)} fusion(f32[256,1,8,128]{0,3,2,1:T(8,128)S(1)} %get-tuple-element.16, f32[256,1,8,128]{0,3,2,1:T(8,128)S(1)} %get-tuple-element.17, f32[1,128,2,128]{1,3,2,0:T(8,128)S(1)} %copy-done.2, f32[1,128,2,128]{1,3,2,0:T(8,128)S(1)} %get-tuple-element.30), kind=kOutput, calls=%fused_computation.32 | convolution fusion | flops 1611202560 | bytes 4456448 | tf_op jit(solution)/shard_map/cqjm,qmpb->cpjb/dot_general | solution.py:17
  66.2 3.6 %fusion.25 = f32[256,2,8,128]{3,0,1,2:T(8,128)S(1)} fusion(f32[256,1,8,128]{0,3,2,1:T(8,128)S(1)} %get-tuple-element.3, f32[256,1,8,128]{0,3,2,1:T(8,128)S(1)} %get-tuple-element.2, f32[1,128,2,128]{1,3,2,0:T(8,128)S(1)} %copy-done.2, f32[1,128,2,128]{1,3,2,0:T(8,128)S(1)} %get-tuple-element.30), kind=kOutput, calls=%fused_computation.33 | convolution fusion | flops 1611202560 | bytes 4456448 | tf_op jit(solution)/shard_map/cqjm,qmpb->cpjb/dot_general | solution.py:17
  71.2 2.4 %fusion.28 = f32[256,128,8]{1,2,0:T(8,128)S(1)} fusion(f32[256,2,8,128]{3,0,1,2:T(8,128)S(1)} %pad_maximum_fusion, f32[4,8]{1,0:T(4,128)S(1)} %copy-done.5, f32[4,8]{1,0:T(4,128)S(1)} %copy-done.7, f32[4,8]{1,0:T(4,128)S(1)} %copy-done.4), kind=kOutput, calls=%fused_computation.34 | convolution fusion | flops 50594176 | bytes 3146112 | tf_op jit(solution)/shard_map/aj,cjb->cab/dot_general | solution.py:17
  75.2 1.5 %copy.77 = f32[256,1,4,128]{0,1,3,2:T(1,128)S(1)} copy(f32[256,1,4,128]{3,2,1,0:T(4,128)} %get-tuple-element.25) | data formatting | bytes 1048576 | tf_op jit(solution)/shard_map/slice | solution.py:118
  76.7 2.9 %fusion.37 = f32[1,256,512]{1,0,2:T(1,128)} fusion(f32[256,1,4,128]{0,1,3,2:T(1,128)S(1)} %copy.77, f32[256,1,4,128]{0,1,3,2:T(1,128)S(1)} %copy.76, f32[512]{0:T(512)S(1)} %bitcast.158, f32[512]{0:T(512)S(1)} %copy-done.6), kind=kLoop, calls=%fused_computation.56 | loop fusion | flops 393216 | bytes 1576960 | tf_op jit(solution)/shard_map/add | solution.py:118
  79.6 3.5 %all-to-all-start.1 = ((f32[1,256,512]{1,0,2:T(1,128)}), f32[1,256,512]{1,0,2:T(1,128)S(1)}, u32[]{:S(2)}, u32[]{:S(2)}) async-start(f32[1,256,512]{1,0,2:T(1,128)} %fusion.37), calls=%async_computation.1 | async-start | bytes 1048576 | tf_op jit(solution)/shard_map/all_to_all | solution.py:121
  83.3 2.4 %fusion.34 = f32[256,4,128]{2,1,0:T(4,128)S(1)} fusion(f32[256,2,8,128]{3,0,1,2:T(8,128)S(1)} %pad_maximum_fusion.1, f32[4,8]{1,0:T(4,128)S(1)} %copy-done.4, f32[4,8]{1,0:T(4,128)S(1)} %copy-done.5), kind=kOutput, calls=%fused_computation.36 | convolution fusion | flops 25296960 | bytes 2621696 | tf_op jit(solution)/shard_map/aj,cjb->cab/dot_general | solution.py:17
  86.7 10.3 %all-to-all-done.1 = f32[1,256,512]{1,0,2:T(1,128)S(1)} async-done(((f32[1,256,512]{1,0,2:T(1,128)}), f32[1,256,512]{1,0,2:T(1,128)S(1)}, u32[]{:S(2)}, u32[]{:S(2)}) %all-to-all-start.1) | async-done | bytes 524320 | tf_op jit(solution)/shard_map/all_to_all | solution.py:121
  98.1 18.8 %all-reduce.2.cloned.1.call-done = f32[1,256,512]{2,1,0:T(8,128)} async-done(((f32[1,256,512]{2,1,0:T(8,128)}), f32[1,256,512]{2,1,0:T(8,128)}) %all-reduce.2.cloned.1.call-update) | async-done | bytes 524304 | tf_op jit(solution)/shard_map/psum | solution.py:129
  116.9 1.9 %copy.150 = f32[1,256,512]{2,1,0:T(8,128)} copy(f32[1,256,512]{2,1,0:T(8,128)} %all-reduce.2.cloned.1.call-done) | data formatting | bytes 1048576
  (48 shorter events, 15.3 us)
Async XLA Ops:
  7.2 20.8 %all-to-all-start = ((f32[4,256,128]{2,1,0:T(8,128)}), f32[4,256,128]{2,1,0:T(8,128)S(1)}, u32[]{:S(2)}, u32[]{:S(2)}) async-start(f32[4,256,128]{2,1,0:T(8,128)} %bitcast.152), calls=%async_computation | async-start | bytes 1048576 | tf_op jit(solution)/shard_map/all_to_all | solution.py:150
  13.6 0.6 copy-start.3
  28.0 8.3 %copy-start.1 = (f32[4,256,128]{2,1,0:T(8,128)}, f32[4,256,128]{2,1,0:T(8,128)S(1)}, u32[]{:S(2)}) copy-start(f32[4,256,128]{2,1,0:T(8,128)S(1)} %all-to-all-done) | copy-start | bytes 1572868
  28.0 18.3 %all-to-all-start.2 = ((f32[4,256,128]{2,1,0:T(8,128)}), f32[4,256,128]{2,1,0:T(8,128)}, u32[]{:S(2)}, u32[]{:S(2)}) async-start(f32[4,256,128]{2,1,0:T(8,128)} %bitcast.153), calls=%async_computation.2 | async-start | bytes 1048576 | tf_op jit(solution)/shard_map/all_to_all | solution.py:149
  53.2 1.2 copy-start
  61.7 0.9 copy-start.2
  70.5 0.7 copy-start.4
  70.5 0.7 copy-start.5
  70.5 0.7 copy-start.7
  73.6 3.1 %copy-start.6 = (f32[512]{0:T(512)S(1)}, f32[512]{0:T(512)}, u32[]{:S(2)}) copy-start(f32[512]{0:T(512)} %broadcast_subtract_fusion.1) | copy-start | bytes 6148
  79.6 17.5 %all-to-all-start.1 = ((f32[1,256,512]{1,0,2:T(1,128)}), f32[1,256,512]{1,0,2:T(1,128)S(1)}, u32[]{:S(2)}, u32[]{:S(2)}) async-start(f32[1,256,512]{1,0,2:T(1,128)} %fusion.37), calls=%async_computation.1 | async-start | bytes 1048576 | tf_op jit(solution)/shard_map/all_to_all | solution.py:121
  83.0 33.9 %all-reduce.2.cloned.1.call-start = ((), (), s32[]{:S(2)}) async-start(), calls=%async_computation.3 | async-start | bytes 1048576 | tf_op jit(solution)/shard_map/psum | solution.py:129
Sparse Core Ops, SparseCore 0:
  86.8 30.0 all-reduce.1
where the time goes:
time: 126 us
  waiting for transfers between devices  46.7 us (37%)
  matrix products  23.7 us (19%)
  local copies, waits for them, and re-layouts  16.1 us (13%)
  between operations  14.3 us (11%)
  starting transfers between devices  14.2 us (11%)
  other arithmetic  10.5 us (8%)
    dot_general x10, matrix products, contract(): jnp.einsum(formula, left_part, right_part, precision=lax.Precision.HIGHES...  23.7 us
    psum x1, waiting for transfers between devices, sum_filter_grad(): return lax.psum(signal_re.reshape(1, chan_count, -1), 'rep')  18.8 us
    all_to_all x1, waiting for transfers between devices, return_grad(): lax.all_to_all(pieces, 'seq', split_axis=2, concat_axis=0, tiled=True)  10.3 us
    all_to_all x1, waiting for transfers between devices, body(): lax.all_to_all(grad_pieces, 'seq', split_axis=0, concat_axis=2, tiled=True)  9.36 us
    all_to_all x1, waiting for transfers between devices, body(): lax.all_to_all(act_pieces, 'seq', split_axis=0, concat_axis=2, tiled=True)  8.21 us
    all_to_all x1, starting transfers between devices, body(): lax.all_to_all(grad_pieces, 'seq', split_axis=0, concat_axis=2, tiled=True)  6.36 us
    unnamed x18, local copies, waits for them, and re-layouts  4.41 us
    all_to_all x1, starting transfers between devices, body(): lax.all_to_all(act_pieces, 'seq', split_axis=0, concat_axis=2, tiled=True)  4.32 us
  transfers between devices with their start and end apart: 4, of which 4 were waited for; matrix products, arithmetic and copies ran while one was open for 12% of the time, Pallas kernels for 0%

commit v1 on v0

--- a/solution.py
+++ b/solution.py
@@ -126,7 +126,7 @@
     product = conj_product(act_spec, grad_spec)
     signal_re = inverse_signal(product, tables, False)
     chan_count = signal_re.shape[0]
-    return lax.psum(signal_re.reshape(1, chan_count, -1), "rep")
+    return jnp.sum(lax.all_gather(signal_re.reshape(1, chan_count, -1), "rep"), axis=0)
 
 
 def body(inputs, out_grad, filters, segment_ids):

time: 126 us -> 108 us (0.86)
  waiting for transfers between devices: 46.7 us -> 17.5 us
  blocking collectives: 0 us -> 16.4 us
  starting transfers between devices: 14.2 us -> 10.7 us
  local copies, waits for them, and re-layouts: 16.1 us -> 13.1 us
    psum x1 -> x0, waiting for transfers between devices: 18.8 us -> none  [sum_filter_grad(): return lax.psum(signal_re.reshape(1, chan_count, -1), 'rep')]
    all_to_all x0 -> x1, blocking collectives: none -> 16.4 us  [return_grad(): lax.all_to_all(pieces, 'seq', split_axis=2, concat_axis=0, tiled=True)]
    all_to_all x1 -> x0, waiting for transfers between devices: 10.3 us -> none  [return_grad(): lax.all_to_all(pieces, 'seq', split_axis=2, concat_axis=0, tiled=True)]
    all_to_all x1 -> x0, starting transfers between devices: 3.47 us -> none  [return_grad(): lax.all_to_all(pieces, 'seq', split_axis=2, concat_axis=0, tiled=True)]
    reduce_sum x0 -> x1, other arithmetic: none -> 2.15 us  [sum_filter_grad(): jnp.sum(lax.all_gather(signal_re.reshape(1, chan_count, -1), 'rep'), axis=0)]
    slice x3, local copies, waits for them, and re-layouts: 3.07 us -> 1.39 us  [return_grad(): grad_full = first_mask * back[:, 0] + second_mask * back[:, 1]]
    unnamed x18 -> x17, local copies, waits for them, and re-layouts: 4.41 us -> 3.04 us
  transfers between devices with their start and end apart: 4 -> 3, of which waited for: 4 -> 2; matrix products, arithmetic and copies ran while one was open for 12% -> 16% of each run, Pallas kernels for 0% -> 0%
where the time goes in v1:
time: 108 us
  matrix products  23.9 us (22%)
  waiting for transfers between devices  17.5 us (16%)
  blocking collectives  16.4 us (15%)
  between operations  14.3 us (13%)
  local copies, waits for them, and re-layouts  13.1 us (12%)
  other arithmetic  11.7 us (11%)
  starting transfers between devices  10.7 us (10%)
    dot_general x10, matrix products, contract(): jnp.einsum(formula, left_part, right_part, precision=lax.Precision.HIGHES...  23.9 us
    all_to_all x1, blocking collectives, return_grad(): lax.all_to_all(pieces, 'seq', split_axis=2, concat_axis=0, tiled=True)  16.4 us
    all_to_all x1, waiting for transfers between devices, body(): lax.all_to_all(grad_pieces, 'seq', split_axis=0, concat_axis=2, tiled=True)  9.36 us
    all_to_all x1, waiting for transfers between devices, body(): lax.all_to_all(act_pieces, 'seq', split_axis=0, concat_axis=2, tiled=True)  8.15 us
    all_to_all x1, starting transfers between devices, body(): lax.all_to_all(grad_pieces, 'seq', split_axis=0, concat_axis=2, tiled=True)  6.36 us
    all_to_all x1, starting transfers between devices, body(): lax.all_to_all(act_pieces, 'seq', split_axis=0, concat_axis=2, tiled=True)  4.13 us
    unnamed x17, local copies, waits for them, and re-layouts  3.04 us
  transfers between devices with their start and end apart: 3, of which 2 were waited for; matrix products, arithmetic and copies ran while one was open for 16% of the time, Pallas kernels for 0%

profile of v1, /device:TPU:0, one launch (start us, length us, event | category | flops | bytes accessed | tf_op | source)
XLA Modules:
  0.0 107.8 jit_solution(15885615457394658844)
XLA Ops:
  7.2 6.4 %all-to-all-start = ((f32[4,256,128]{2,1,0:T(8,128)}), f32[4,256,128]{2,1,0:T(8,128)S(1)}, u32[]{:S(2)}, u32[]{:S(2)}) async-start(f32[4,256,128]{2,1,0:T(8,128)} %bitcast.153), calls=%async_computation | async-start | bytes 1048576 | tf_op jit(solution)/shard_map/all_to_all | solution.py:150
  14.2 1.2 %reshape_squeeze.3 = f32[256,4,128]{2,1,0:T(4,128)S(1)} reshape(f32[1,256,512]{2,1,0:T(8,128)} %param.6) | data formatting | bytes 1048576 | tf_op jit(solution)/shard_map/reshape;squeeze | solution.py:144
  16.8 1.9 %convolution_bitcast_fusion = f32[256,2,8,128]{3,2,1,0:T(8,128)S(1)} fusion(f32[256,4,128]{2,1,0:T(4,128)S(1)} %reshape_squeeze.3, f32[16,8]{0,1:T(8,128)S(1)} %maximum_maximum_fusion), kind=kOutput, calls=%fused_computation.26 | convolution fusion | flops 25165824 | bytes 2623488 | tf_op jit(solution)/shard_map/ja,cab->cjb/dot_general | solution.py:17
  18.7 9.4 %all-to-all-done = f32[4,256,128]{2,1,0:T(8,128)S(1)} async-done(((f32[4,256,128]{2,1,0:T(8,128)}), f32[4,256,128]{2,1,0:T(8,128)S(1)}, u32[]{:S(2)}, u32[]{:S(2)}) %all-to-all-start) | async-done | bytes 524320 | tf_op jit(solution)/shard_map/all_to_all | solution.py:150
  28.0 4.1 %all-to-all-start.2 = ((f32[4,256,128]{2,1,0:T(8,128)}), f32[4,256,128]{2,1,0:T(8,128)}, u32[]{:S(2)}, u32[]{:S(2)}) async-start(f32[4,256,128]{2,1,0:T(8,128)} %bitcast.154), calls=%async_computation.2 | async-start | bytes 1048576 | tf_op jit(solution)/shard_map/all_to_all | solution.py:149
  33.8 1.3 %copy.72 = f32[4,8]{1,0:T(4,128)} copy(f32[4,8]{0,1:T(8,128)} %bitcast.161) | data formatting | bytes 256 | tf_op jit(solution)/shard_map/slice | solution.py:38
  37.0 1.2 %fusion.88 = (f32[256,1,8,128]{3,2,1,0:T(8,128)S(1)}, f32[256,1,8,128]{3,2,1,0:T(8,128)}) fusion(f32[256,2,8,128]{3,2,1,0:T(8,128)S(1)} %convolution_bitcast_fusion), kind=kLoop, calls=%fused_computation.134 | loop fusion | bytes 4194304 | tf_op jit(solution)/shard_map/slice | solution.py:67
  38.1 8.2 %all-to-all-done.2 = f32[4,256,128]{2,1,0:T(8,128)} async-done(((f32[4,256,128]{2,1,0:T(8,128)}), f32[4,256,128]{2,1,0:T(8,128)}, u32[]{:S(2)}, u32[]{:S(2)}) %all-to-all-start.2) | async-done | bytes 524320 | tf_op jit(solution)/shard_map/all_to_all | solution.py:149
  46.3 1.5 %bitcast_multiply_fusion.5 = (f32[256,1,4,128]{3,0,2,1:T(8,128)S(1)}, f32[256,1,4,128]{3,0,2,1:T(8,128)S(1)}, f32[256,1,4,128]{3,0,2,1:T(8,128)S(1)}, f32[256,1,4,128]{3,0,2,1:T(8,128)S(1)}) fusion(f32[4,256,128]{2,1,0:T(8,128)} %copy-done.1, f32[4,128]{1,0:T(4,128)} %broadcast_subtract_fusion, f32[4,128]{1,0:T(4,128)S(1)} %bitcast.159, ...), kind=kLoop, calls=%fused_computation.59 | loop fusion | flops 524288 | bytes 3149824 | tf_op jit(solution)/shard_map/mul | solution.py:111
  48.6 1.8 %convolution_bitcast_fusion.2 = f32[256,2,8,128]{3,2,1,0:T(8,128)S(1)} fusion(f32[256,8,128]{2,1,0:T(8,128)S(1)} %bitcast.151, f32[16,8]{0,1:T(8,128)S(1)} %maximum_maximum_fusion), kind=kOutput, calls=%fused_computation.31 | convolution fusion | flops 50331648 | bytes 3146240 | tf_op jit(solution)/shard_map/ja,cab->cjb/dot_general | solution.py:17
  51.3 1.8 %convolution_bitcast_fusion.1 = f32[256,2,8,128]{3,2,1,0:T(8,128)S(1)} fusion(f32[256,8,128]{2,1,0:T(8,128)S(1)} %bitcast.150, f32[16,8]{0,1:T(8,128)S(1)} %maximum_maximum_fusion), kind=kOutput, calls=%fused_computation.30 | convolution fusion | flops 50331648 | bytes 3146240 | tf_op jit(solution)/shard_map/ja,cab->cjb/dot_general | solution.py:17
  53.3 1.1 copy-done
  54.4 1.2 %multiply_subtract_fusion.2 = (f32[256,1,8,128]{3,0,1,2:T(8,128)S(1)}, f32[256,1,8,128]{3,0,1,2:T(8,128)S(1)}, f32[256,1,8,128]{3,0,1,2:T(8,128)S(1)}, f32[256,1...) fusion(f32[256,1,8,128]{3,2,1,0:T(8,128)S(1)} %get-tuple-element.19, ...), kind=kLoop, calls=%fused_computation.44 | loop fusion | flops 4718592 | bytes 12591104 | tf_op jit(solution)/shard_map/sub | solution.py:71
  55.6 2.0 %fusion.21 = f32[256,2,8,128]{0,3,2,1:T(8,128)S(1)} fusion(f32[256,1,8,128]{3,0,1,2:T(8,128)S(1)} %get-tuple-element.40, f32[256,1,8,128]{3,0,1,2:T(8,128)S(1)} %get-tuple-element.41, f32[1,128,2,128]{1,3,0,2:T(8,128)S(1)} %get-tuple-element.31, f32[1,128,2,128]{1,3,0,2:T(8,128)S(1)} %get-tuple-element.34), kind=kOutput, calls=%fused_computation.29 | convolution fusion | flops 1611202560 | bytes 4456448 | tf_op jit(solution)/shard_map/cpjb,pbqm->cqjm/dot_general | solution.py:17
  57.5 2.0 %fusion.20 = f32[256,2,8,128]{0,3,2,1:T(8,128)S(1)} fusion(f32[256,1,8,128]{3,0,1,2:T(8,128)S(1)} %get-tuple-element.38, f32[256,1,8,128]{3,0,1,2:T(8,128)S(1)} %get-tuple-element.39, f32[1,128,2,128]{1,3,0,2:T(8,128)S(1)} %get-tuple-element.31, f32[1,128,2,128]{1,3,0,2:T(8,128)S(1)} %get-tuple-element.34), kind=kOutput, calls=%fused_computation.28 | convolution fusion | flops 1611202560 | bytes 4456448 | tf_op jit(solution)/shard_map/cpjb,pbqm->cqjm/dot_general | solution.py:17
  59.5 2.2 %fusion.19 = f32[256,2,8,128]{0,3,2,1:T(8,128)S(1)} fusion(f32[256,1,8,128]{3,0,1,2:T(8,128)S(1)} %get-tuple-element.9, f32[256,1,8,128]{3,0,1,2:T(8,128)S(1)} %get-tuple-element.8, f32[1,128,2,128]{1,3,0,2:T(8,128)S(1)} %get-tuple-element.31, f32[1,128,2,128]{1,3,0,2:T(8,128)S(1)} %get-tuple-element.34), kind=kOutput, calls=%fused_computation.27 | convolution fusion | flops 1611202560 | bytes 4456448 | tf_op jit(solution)/shard_map/cpjb,pbqm->cqjm/dot_general | solution.py:17
  62.6 3.6 %fusion.22 = f32[256,2,8,128]{3,0,1,2:T(8,128)S(1)} fusion(f32[256,1,8,128]{0,3,2,1:T(8,128)S(1)} %get-tuple-element.16, f32[256,1,8,128]{0,3,2,1:T(8,128)S(1)} %get-tuple-element.17, f32[1,128,2,128]{1,3,2,0:T(8,128)S(1)} %copy-done.2, f32[1,128,2,128]{1,3,2,0:T(8,128)S(1)} %get-tuple-element.30), kind=kOutput, calls=%fused_computation.32 | convolution fusion | flops 1611202560 | bytes 4456448 | tf_op jit(solution)/shard_map/cqjm,qmpb->cpjb/dot_general | solution.py:17
  66.2 3.6 %fusion.25 = f32[256,2,8,128]{3,0,1,2:T(8,128)S(1)} fusion(f32[256,1,8,128]{0,3,2,1:T(8,128)S(1)} %get-tuple-element.3, f32[256,1,8,128]{0,3,2,1:T(8,128)S(1)} %get-tuple-element.2, f32[1,128,2,128]{1,3,2,0:T(8,128)S(1)} %copy-done.2, f32[1,128,2,128]{1,3,2,0:T(8,128)S(1)} %get-tuple-element.30), kind=kOutput, calls=%fused_computation.33 | convolution fusion | flops 1611202560 | bytes 4456448 | tf_op jit(solution)/shard_map/cqjm,qmpb->cpjb/dot_general | solution.py:17
  71.2 2.4 %fusion.34 = f32[256,4,128]{2,1,0:T(4,128)S(1)} fusion(f32[256,2,8,128]{3,0,1,2:T(8,128)S(1)} %pad_maximum_fusion.1, f32[4,8]{1,0:T(4,128)S(1)} %copy-done.4, f32[4,8]{1,0:T(4,128)S(1)} %copy-done.5), kind=kOutput, calls=%fused_computation.36 | convolution fusion | flops 25296960 | bytes 2621696 | tf_op jit(solution)/shard_map/aj,cjb->cab/dot_general | solution.py:17
  73.6 1.0 all_gather_reshape_reshape.3
  75.3 2.6 %fusion.28 = f32[256,128,8]{1,2,0:T(8,128)S(1)} fusion(f32[256,2,8,128]{3,0,1,2:T(8,128)S(1)} %pad_maximum_fusion, f32[4,8]{1,0:T(4,128)S(1)} %copy-done.5, f32[4,8]{1,0:T(4,128)S(1)} %copy-done.7, f32[4,8]{1,0:T(4,128)S(1)} %copy-done.4), kind=kOutput, calls=%fused_computation.34 | convolution fusion | flops 50594176 | bytes 3146112 | tf_op jit(solution)/shard_map/aj,cjb->cab/dot_general | solution.py:17
  79.4 1.9 %fusion.37 = f32[1,256,512]{1,0,2:T(1,128)S(1)} fusion(f32[256,1,4,128]{0,1,3,2:T(1,128)S(1)} %copy.77, f32[256,1,4,128]{0,1,3,2:T(1,128)S(1)} %copy.76, f32[512]{0:T(512)S(1)} %bitcast.160, f32[512]{0:T(512)S(1)} %copy-done.6), kind=kLoop, calls=%fused_computation.56 | loop fusion | flops 393216 | bytes 1576960 | tf_op jit(solution)/shard_map/add | solution.py:118
  81.3 16.4 %all_to_all.45 = f32[1,256,512]{1,0,2:T(1,128)S(1)} all-to-all(f32[1,256,512]{1,0,2:T(1,128)S(1)} %fusion.37), channel_id=1, replica_groups=mesh['seq'=4,'chan'=4,'rep'=2] {'seq'}, dimensions={2} | all-to-all | bytes 1048576 | tf_op jit(solution)/shard_map/all_to_all | solution.py:121
  98.8 2.1 %reduce_sum.11 = f32[256,512]{1,0:T(8,128)} reduce(f32[2,1,256,512]{3,2,1,0:T(8,128)} %all-gather.2.cloned.1.call-done, f32[]{:T(128)} %constant.55.clone.1), dimensions={0,1}, to_apply=%region_0.1 | reduce | flops 131072 | bytes 1572868 | tf_op jit(solution)/shard_map/reduce_sum | solution.py:129
  (47 shorter events, 12.5 us)
Async XLA Ops:
  7.2 20.8 %all-to-all-start = ((f32[4,256,128]{2,1,0:T(8,128)}), f32[4,256,128]{2,1,0:T(8,128)S(1)}, u32[]{:S(2)}, u32[]{:S(2)}) async-start(f32[4,256,128]{2,1,0:T(8,128)} %bitcast.153), calls=%async_computation | async-start | bytes 1048576 | tf_op jit(solution)/shard_map/all_to_all | solution.py:150
  13.6 0.6 copy-start.3
  28.0 8.4 %copy-start.1 = (f32[4,256,128]{2,1,0:T(8,128)}, f32[4,256,128]{2,1,0:T(8,128)S(1)}, u32[]{:S(2)}) copy-start(f32[4,256,128]{2,1,0:T(8,128)S(1)} %all-to-all-done) | copy-start | bytes 1572868
  28.0 18.2 %all-to-all-start.2 = ((f32[4,256,128]{2,1,0:T(8,128)}), f32[4,256,128]{2,1,0:T(8,128)}, u32[]{:S(2)}, u32[]{:S(2)}) async-start(f32[4,256,128]{2,1,0:T(8,128)} %bitcast.154), calls=%async_computation.2 | async-start | bytes 1048576 | tf_op jit(solution)/shard_map/all_to_all | solution.py:149
  32.2 66.6 %all-gather.2.cloned.1.call-start = ((), (), s32[]{:S(2)}) async-start(), calls=%async_computation.3 | async-start | bytes 1572864 | tf_op jit(solution)/shard_map/all_gather | solution.py:129
  53.2 1.2 %copy-start = (f32[256,1,8,128]{3,2,1,0:T(8,128)S(1)}, f32[256,1,8,128]{3,2,1,0:T(8,128)}, u32[]{:S(2)}) copy-start(f32[256,1,8,128]{3,2,1,0:T(8,128)} %get-tuple-element.23) | copy-start | bytes 3145732
  61.7 0.9 copy-start.2
  70.5 0.7 copy-start.4
  70.5 0.7 copy-start.5
  74.6 0.7 copy-start.7
  77.9 1.4 %copy-start.6 = (f32[512]{0:T(512)S(1)}, f32[512]{0:T(512)}, u32[]{:S(2)}) copy-start(f32[512]{0:T(512)} %broadcast_subtract_fusion.1) | copy-start | bytes 6148
Sparse Core Ops, SparseCore 0:
  74.7 20.3 all-gather.1
